TPU v7x, 32 devices: a whole 2x2x4 slice. The times are simulated.
32 devices in a mesh: dp: 2 (over y), seq: 4 (over z), tensor: 4 (over x, core).
Axes of the slice: x: 2, y: 2, z: 4, core: 2. Of those that a mesh axis runs over, the one named last changes fastest.
Arguments:
- layer_input: bfloat16 [6, 1024, 2048], P('dp', 'seq'), may hold values from -6 to 6
- lengths: int32 [6], P('dp'), may hold values from 256 to 1024, as said below
- cotangent: bfloat16 [6, 1024, 2048], P('dp', ('seq', 'tensor')), may hold values from -6 to 6
- ln1_gain: bfloat16 [2048], replicated, may hold values from 0.5 to 1.5
- ln1_bias: bfloat16 [2048], replicated, may hold values from -3 to 3
- w_query: bfloat16 [2048, 2048], P(None, 'tensor'), may hold values from -0.125 to 0.125
- b_query: bfloat16 [2048], P('tensor'), may hold values from -3 to 3
- w_kv: bfloat16 [2048, 256], replicated, may hold values from -0.125 to 0.125
- b_value: bfloat16 [128], replicated, may hold values from -3 to 3
- w_out: bfloat16 [2048, 2048], P('tensor'), may hold values from -0.5 to 0.5
- b_out: bfloat16 [2048], replicated, may hold values from -3 to 3
- ln2_gain: bfloat16 [2048], replicated, may hold values from 0.5 to 1.5
- ln2_bias: bfloat16 [2048], replicated, may hold values from -3 to 3
- w_up: bfloat16 [2048, 8192], P(None, 'tensor'), may hold values from -0.125 to 0.125
- b_up: bfloat16 [8192], P('tensor'), may hold values from -3 to 3
- w_down: bfloat16 [8192, 2048], P('tensor'), may hold values from -0.0625 to 0.0625
- b_down: bfloat16 [2048], replicated, may hold values from -3 to 3
Outputs:
- layer_output: bfloat16 [6, 1024, 2048], P('dp', ('seq', 'tensor'))
- input_grad: float32 [6, 1024, 2048], P('dp', ('seq', 'tensor'))
- g_w_query: float32 [2048, 2048], P(('dp', 'seq'), 'tensor')
- g_b_query: float32 [16, 128], P('tensor', ('dp', 'seq'))
- g_w_kv: float32 [2048, 256], P(('dp', 'seq', 'tensor'))
- g_b_value: float32 [128], P(('dp', 'seq', 'tensor'))
- g_w_out: float32 [2048, 2048], P('tensor', ('dp', 'seq'))
- g_w_up: float32 [2048, 8192], P(('dp', 'seq'), 'tensor')
- g_b_up: float32 [64, 128], P('tensor', ('dp', 'seq'))
- g_w_down: float32 [8192, 2048], P('tensor', ('dp', 'seq'))
- g_norms_biases: float32 [6, 2048], P(None, ('dp', 'seq', 'tensor'))
Inputs may be any that keep to these rules, and one draw needn't show every extreme that they name: `lengths`: the number of real tokens at the start of each row; the rest of the row is padding.
All inputs are finite; a program needn't handle non-finite values.
Results may differ from a plain program's by a relative error of at most 0.012.
Values may be sent and summed in bfloat16 or wider, within the bound.
A program may use at most 256 MiB of HBM per device.

v0:
```python
import math
import jax
import jax.numpy as jnp
from jax import lax
from jax.sharding import PartitionSpec as P

NORM_EPS = 1e-05


def normalize(values_in):
    row_mean = jnp.mean(values_in, -1, keepdims=True)
    centered = values_in - row_mean
    variance = jnp.mean(centered * centered, -1, keepdims=True)
    inv_std = lax.rsqrt(variance + NORM_EPS)
    return (centered * inv_std, inv_std)


def norm_back(grad_in, normed, inv_std, norm_gain):
    scaled = grad_in * norm_gain
    mean_scaled = jnp.mean(scaled, -1, keepdims=True)
    mean_mixed = jnp.mean(scaled * normed, -1, keepdims=True)
    return inv_std * (scaled - mean_scaled - normed * mean_mixed)


def across_rows(left_in, right_in):
    return lax.dot_general(
        left_in, right_in, (((0,), (0,)), ((), ())), preferred_element_type=jnp.float32
    )


def times_transposed(left_in, right_in):
    return lax.dot_general(
        left_in, right_in, (((1,), (1,)), ((), ())), preferred_element_type=jnp.float32
    )


def shards(
    layer_input,
    lengths,
    cotangent,
    ln1_gain,
    ln1_bias,
    w_query,
    b_query,
    w_kv,
    b_value,
    w_out,
    b_out,
    ln2_gain,
    ln2_bias,
    w_up,
    b_up,
    w_down,
    b_down,
):
    n_rows, seq_len, model_width = layer_input.shape
    share_len = seq_len // lax.axis_size("tensor")
    tensor_index = lax.axis_index("tensor")
    seq_index = lax.axis_index("seq")
    full_len = seq_len * lax.axis_size("seq")
    head_size = w_kv.shape[1] // 2
    num_heads = w_query.shape[1] // head_size
    q_scale = 1.0 / math.sqrt(head_size)

    def own_rows(values_in):
        return lax.dynamic_slice_in_dim(values_in, tensor_index * share_len, share_len, 1)

    positions = seq_index * seq_len + jnp.arange(seq_len, dtype=jnp.int32)
    key_places = jnp.arange(full_len, dtype=jnp.int32)
    is_valid = (positions[None, :] < lengths[:, None]).astype(jnp.float32)
    allowed_keys = (key_places[None, None, :] <= positions[None, :, None]) & (
        key_places[None, None, :] < lengths[:, None, None]
    )
    valid_own = own_rows(is_valid)
    x_float = layer_input.astype(jnp.float32)
    normed_x1, inv_one = normalize(x_float)
    normed_one = (normed_x1 * ln1_gain + ln1_bias).astype(jnp.bfloat16)
    flat_one = normed_one.reshape(n_rows * seq_len, model_width)
    queries = (
        (jnp.dot(flat_one, w_query, preferred_element_type=jnp.float32) + b_query) * q_scale
    ).astype(jnp.bfloat16)
    queries = queries.reshape(n_rows, seq_len, num_heads, head_size)
    kv_bias = jnp.concatenate([jnp.zeros((head_size,), jnp.float32), b_value.astype(jnp.float32)])
    kv_local = (jnp.dot(flat_one, w_kv, preferred_element_type=jnp.float32) + kv_bias).astype(
        jnp.bfloat16
    )
    kv_local = kv_local.reshape(n_rows, seq_len, 2 * head_size)
    kv_all = lax.all_gather(kv_local, "seq", axis=1, tiled=True)
    key_rows = kv_all[..., :head_size]
    value_rows = kv_all[..., head_size:]

    def scores_of(query_rows):
        raw_scores = jnp.einsum(
            "rshd,rld->rhsl", query_rows, key_rows, preferred_element_type=jnp.float32
        )
        return jnp.where(allowed_keys[:, None], raw_scores, -1e30)

    scores = scores_of(queries)
    row_max = jnp.max(scores, -1, keepdims=True)
    exp_scores = jnp.exp(scores - row_max)
    exp_total = jnp.sum(exp_scores, -1, keepdims=True)
    soft_probs = exp_scores / exp_total
    log_total = row_max + jnp.log(exp_total)
    mixed_heads = jnp.einsum(
        "rhsl,rld->rshd",
        soft_probs.astype(jnp.bfloat16),
        value_rows,
        preferred_element_type=jnp.float32,
    ).astype(jnp.bfloat16)
    mixed_heads = mixed_heads.reshape(n_rows * seq_len, num_heads * head_size)
    attn_part = jnp.dot(mixed_heads, w_out, preferred_element_type=jnp.float32).reshape(
        n_rows, seq_len, model_width
    )
    residual = x_float + (lax.psum(attn_part, "tensor") + b_out)
    normed_x2, inv_two = normalize(residual)
    normed_two = (normed_x2 * ln2_gain + ln2_bias).astype(jnp.bfloat16)
    resid_own = own_rows(residual)
    normed_x2_own = own_rows(normed_x2)
    flat_two = normed_two.reshape(n_rows * seq_len, model_width)
    pre_act = jnp.dot(flat_two, w_up, preferred_element_type=jnp.float32) + b_up
    activated, gelu_pull = jax.vjp(
        lambda inner_in: jax.nn.gelu(inner_in, approximate=True), pre_act
    )
    act_low = activated.astype(jnp.bfloat16)
    mlp_part = jnp.dot(act_low, w_down, preferred_element_type=jnp.float32).reshape(
        n_rows, seq_len, model_width
    )
    mlp_own = (
        lax.psum_scatter(
            mlp_part.astype(jnp.bfloat16), "tensor", scatter_dimension=1, tiled=True
        ).astype(jnp.float32)
        + b_down
    )
    y_own = (valid_own[..., None] * (resid_own + mlp_own)).astype(jnp.bfloat16)
    cot_full = lax.all_gather(cotangent, "tensor", axis=1, tiled=True)
    grad_y = cot_full.astype(jnp.float32) * is_valid[..., None]
    grad_y_low = grad_y.astype(jnp.bfloat16).reshape(n_rows * seq_len, model_width)
    grad_y_own = cotangent.astype(jnp.float32) * valid_own[..., None]
    g_w_down = across_rows(act_low, grad_y_low)
    grad_act = times_transposed(grad_y_low, w_down)
    grad_pre = gelu_pull(grad_act)[0].astype(jnp.bfloat16)
    g_w_up = across_rows(flat_two, grad_pre)
    g_b_up = jnp.sum(grad_pre.astype(jnp.float32), axis=0)
    grad_a2 = times_transposed(grad_pre, w_up).reshape(n_rows, seq_len, model_width)
    grad_n2 = lax.psum(grad_a2, "tensor")
    grad_resid = grad_y + norm_back(grad_n2, normed_x2, inv_two, ln2_gain)
    grad_resid_low = grad_resid.astype(jnp.bfloat16)
    grad_resid_own = own_rows(grad_resid)
    grad_n2_own = own_rows(grad_n2)
    grad_resid_own_low = own_rows(grad_resid_low)
    g_ln2_gain = jnp.sum(grad_n2_own * normed_x2_own, axis=(0, 1))
    g_ln2_bias = jnp.sum(grad_n2_own, axis=(0, 1))
    g_b_out = jnp.sum(grad_resid_own_low.astype(jnp.float32), axis=(0, 1))
    g_b_down = jnp.sum(grad_y_own, axis=(0, 1))
    flat_resid = grad_resid_low.reshape(n_rows * seq_len, model_width)
    g_w_out = across_rows(mixed_heads, flat_resid)
    grad_mixed = times_transposed(flat_resid, w_out).astype(jnp.bfloat16)
    grad_mixed = grad_mixed.reshape(n_rows, seq_len, num_heads, head_size)
    again_probs = jnp.exp(scores_of(queries) - log_total)
    grad_probs = jnp.einsum(
        "rshd,rld->rhsl", grad_mixed, value_rows, preferred_element_type=jnp.float32
    )
    inner_sum = jnp.sum(again_probs * grad_probs, -1, keepdims=True)
    grad_scores = (again_probs * (grad_probs - inner_sum)).astype(jnp.bfloat16)
    grad_query = jnp.einsum(
        "rhsl,rld->rshd", grad_scores, key_rows, preferred_element_type=jnp.float32
    ).astype(jnp.bfloat16)
    grad_keys = jnp.einsum(
        "rhsl,rshd->rld", grad_scores, queries, preferred_element_type=jnp.float32
    )
    grad_values = jnp.einsum(
        "rhsl,rshd->rld",
        again_probs.astype(jnp.bfloat16),
        grad_mixed,
        preferred_element_type=jnp.float32,
    )
    grad_kv = jnp.concatenate([grad_keys, grad_values], -1)
    grad_kv_own = lax.psum_scatter(
        grad_kv, ("seq", "tensor"), scatter_dimension=1, tiled=True
    ).astype(jnp.bfloat16)
    flat_query = grad_query.reshape(n_rows * seq_len, num_heads * head_size)
    g_w_query = across_rows(flat_one, flat_query) * q_scale
    g_b_query = jnp.sum(flat_query.astype(jnp.float32), axis=0) * q_scale
    grad_n1_part = (times_transposed(flat_query, w_query) * q_scale).reshape(
        n_rows, seq_len, model_width
    )
    grad_n1_own = lax.psum_scatter(
        grad_n1_part.astype(jnp.bfloat16), "tensor", scatter_dimension=1, tiled=True
    ).astype(jnp.float32)
    flat_kv = grad_kv_own.reshape(n_rows * share_len, 2 * head_size)
    grad_n1_own = grad_n1_own + times_transposed(flat_kv, w_kv).reshape(
        n_rows, share_len, model_width
    )
    one_own = own_rows(normed_one).reshape(n_rows * share_len, model_width)
    g_w_kv = across_rows(one_own, flat_kv)
    g_b_value = jnp.sum(flat_kv[:, head_size:].astype(jnp.float32), axis=0)
    normed_x1_own = own_rows(normed_x1)
    x_grad_own = grad_resid_own + norm_back(grad_n1_own, normed_x1_own, own_rows(inv_one), ln1_gain)
    g_ln1_gain = jnp.sum(grad_n1_own * normed_x1_own, axis=(0, 1))
    g_ln1_bias = jnp.sum(grad_n1_own, axis=(0, 1))
    query_table = g_b_query.reshape(num_heads, head_size)
    up_table = g_b_up.reshape(-1, 128)
    summed = (
        lax.psum_scatter(g_w_query, ("dp", "seq"), scatter_dimension=0, tiled=True),
        lax.psum_scatter(query_table, ("dp", "seq"), scatter_dimension=1, tiled=True),
        lax.psum_scatter(g_w_out, ("dp", "seq"), scatter_dimension=1, tiled=True),
        lax.psum_scatter(g_w_up, ("dp", "seq"), scatter_dimension=0, tiled=True),
        lax.psum_scatter(up_table, ("dp", "seq"), scatter_dimension=1, tiled=True),
        lax.psum_scatter(g_w_down, ("dp", "seq"), scatter_dimension=1, tiled=True),
    )
    small_grads = jnp.stack([g_ln1_gain, g_ln1_bias, g_ln2_gain, g_ln2_bias, g_b_out, g_b_down])
    shared = (
        lax.psum_scatter(g_w_kv, ("dp", "seq", "tensor"), scatter_dimension=0, tiled=True),
        lax.psum_scatter(small_grads, ("dp", "seq", "tensor"), scatter_dimension=1, tiled=True),
        lax.psum_scatter(g_b_value, ("dp", "seq", "tensor"), scatter_dimension=0, tiled=True),
    )
    return (
        y_own,
        x_grad_own,
        summed[0],
        summed[1],
        shared[0],
        shared[2],
        summed[2],
        summed[3],
        summed[4],
        summed[5],
        shared[1],
    )


def solution(mesh):
    placed = (
        P("dp", "seq", None),
        P("dp"),
        P("dp", ("seq", "tensor"), None),
        P(),
        P(),
        P(None, "tensor"),
        P("tensor"),
        P(),
        P(),
        P("tensor", None),
        P(),
        P(),
        P(),
        P(None, "tensor"),
        P("tensor"),
        P("tensor", None),
        P(),
    )
    return jax.shard_map(
        shards,
        mesh=mesh,
        in_specs=placed,
        out_specs=(
            P("dp", ("seq", "tensor"), None),
            P("dp", ("seq", "tensor"), None),
            P(("dp", "seq"), "tensor"),
            P("tensor", ("dp", "seq")),
            P(("dp", "seq", "tensor"), None),
            P(("dp", "seq", "tensor")),
            P("tensor", ("dp", "seq")),
            P(("dp", "seq"), "tensor"),
            P("tensor", ("dp", "seq")),
            P("tensor", ("dp", "seq")),
            P(None, ("dp", "seq", "tensor")),
        ),
        check_vma=False,
    )
```

profile of v0, /device:TPU:0, one launch (start us, length us, event | category | flops | bytes accessed | tf_op | source)
XLA Modules:
  0.0 1648.8 jit_solution(9399819819224728491)
XLA Ops:
  21.5 5.2 multiply_convert_fusion.3
  30.5 29.8 %all-gather.3.cloned.1.call-done = bf16[3,1024,256]{2,1,0:T(8,128)(2,1)} async-done(((bf16[3,256,256]{2,1,0:T(8,128)(2,1)}), bf16[3,1024,256]{2,1,0:T(8,128)(2,1)}) %all-gather.3.cloned.1.call-update) | async-done | bytes 1572880 | tf_op jit(solution)/shard_map/all_gather | solution.py:88
  60.4 7.9 fusion.4
  68.3 7.4 fusion.3
  75.8 6.5 fusion.28
  93.4 117.9 %all-reduce.7.cloned.1.call-done = f32[3,256,2048]{2,1,0:T(8,128)} async-done(((f32[3,256,2048]{2,1,0:T(8,128)}), f32[3,256,2048]{2,1,0:T(8,128)}) %all-reduce.7.cloned.1.call-update) | async-done | bytes 6291472 | tf_op jit(solution)/shard_map/psum | solution.py:114
  211.3 4.6 fusion.48
  224.9 8.5 fusion.49
  233.4 14.9 convert_reduce_fusion.1
  248.3 8.6 fusion.50
  257.0 13.3 convolution_convert_fusion
  270.3 106.6 %all-reduce.9.cloned.1.call-done = f32[3,256,2048]{2,1,0:T(8,128)} async-done(((f32[3,256,2048]{2,1,0:T(8,128)}), f32[3,256,2048]{2,1,0:T(8,128)}) %all-reduce.9.cloned.1.call-update) | async-done | bytes 6291472 | tf_op jit(solution)/shard_map/psum | solution.py:145
  376.9 5.9 multiply_reduce_fusion.2
  384.2 6.1 fusion.47
  399.3 8.6 fusion
  407.9 6.7 fusion.2
  421.6 5.3 multiply_convert_fusion
  429.4 9.6 fusion.25
  439.0 6.1 convolution_bitcast_fusion.1
  449.8 5.0 copy.69
  454.8 98.2 %all-reduce.10 = bf16[3,1024,256]{2,0,1:T(4,128)(2,1)} all-reduce(f32[3,1024,256]{2,0,1:T(4,128)} %copy.69), channel_id=4, replica_groups=mesh['dp'=2,'seq'=4,'tensor'=4] {'seq','tensor'}, use_global_device_ids=true, to_apply=%region_13.14.clone | all-reduce | flops 786432 | bytes 4718592
  570.2 6.0 fusion.32
  576.3 5.7 convolution_multiply_fusion
  582.3 13.9 fusion.45
  596.3 12.5 fusion.51
  611.0 40.6 %all-reduce.2 = f32[128]{0:T(128)S(1)} all-reduce(f32[128]{0:T(128)S(1)} %convert_reduce_fusion.4), channel_id=8, replica_groups=mesh['dp'=2,'seq'=4,'tensor'=4] {'dp','seq','tensor'}, use_global_device_ids=true, to_apply=%region_21.22.clone | all-reduce | flops 128 | bytes 1024
  657.5 99.5 %reduce-scatter.35.cloned.1.call-done = f32[64,6]{1,0:T(8,128)} async-done(((f32[2048,6]{1,0:T(8,128)}), f32[64,6]{1,0:T(8,128)}) %reduce-scatter.35.cloned.1.call-update) | async-done | bytes 1552
  758.4 135.5 %reduce-scatter.23.cloned.1.call-done = f32[64,256]{1,0:T(8,128)} async-done(((f32[2048,256]{1,0:T(8,128)}), f32[64,256]{1,0:T(8,128)}) %reduce-scatter.23.cloned.1.call-update) | async-done | bytes 65552 | tf_op jit(solution)/shard_map/reduce_scatter | solution.py:213
  893.9 89.4 %reduce-scatter.25.cloned.1.call-done = f32[512,256]{1,0:T(8,128)} async-done(((f32[512,2048]{1,0:T(8,128)}), f32[512,256]{1,0:T(8,128)}) %reduce-scatter.25.cloned.1.call-update) | async-done | bytes 524304 | tf_op jit(solution)/shard_map/reduce_scatter | solution.py:206
  983.4 92.0 %reduce-scatter.21.cloned.1.call-done = f32[256,512]{1,0:T(8,128)} async-done(((f32[2048,512]{1,0:T(8,128)}), f32[256,512]{1,0:T(8,128)}) %reduce-scatter.21.cloned.1.call-update) | async-done | bytes 524304 | tf_op jit(solution)/shard_map/reduce_scatter | solution.py:204
  1075.4 283.5 %reduce-scatter.29.cloned.1.call-done = f32[2048,256]{1,0:T(8,128)} async-done(((f32[2048,2048]{1,0:T(8,128)}), f32[2048,256]{1,0:T(8,128)}) %reduce-scatter.29.cloned.1.call-update) | async-done | bytes 2097168 | tf_op jit(solution)/shard_map/reduce_scatter | solution.py:209
  1358.9 282.9 %reduce-scatter.27.cloned.1.call-done = f32[256,2048]{1,0:T(8,128)} async-done(((f32[2048,2048]{1,0:T(8,128)}), f32[256,2048]{1,0:T(8,128)}) %reduce-scatter.27.cloned.1.call-update) | async-done | bytes 2097168 | tf_op jit(solution)/shard_map/reduce_scatter | solution.py:207
  (164 shorter events, 88.9 us)
Async XLA Ops:
  7.2 76.0 %copy-start = (bf16[512,2048]{1,0:T(8,128)(2,1)S(1)}, bf16[512,2048]{1,0:T(8,128)(2,1)}, u32[]{:S(2)}) copy-start(bf16[512,2048]{1,0:T(8,128)(2,1)} %param.26) | copy-start | bytes 6291460
  7.2 6.4 copy-start.22
  7.2 6.4 copy-start.23
  7.2 53.2 %all-gather.3.cloned.1.call-start = ((), (), s32[]{:S(2)}) async-start(), calls=%async_computation.10 | async-start | bytes 1966080 | tf_op jit(solution)/shard_map/all_gather | solution.py:88
  7.3 6.4 copy-start.3
  20.5 68.9 %all-gather.5.cloned.1.call-start = ((), (), s32[]{:S(2)}) async-start(), calls=%async_computation.13 | async-start | bytes 3932160 | tf_op jit(solution)/shard_map/all_gather | solution.py:135
  21.2 190.1 %all-reduce.7.cloned.1.call-start = ((), (), s32[]{:S(2)}) async-start(), calls=%async_computation.11 | async-start | bytes 12582912 | tf_op jit(solution)/shard_map/psum | solution.py:114
  21.5 8.2 copy-start.29
  68.3 7.5 copy-start.9
  87.7 289.2 %all-reduce.9.cloned.1.call-start = ((), (), s32[]{:S(2)}) async-start(), calls=%async_computation.14 | async-start | bytes 12582912 | tf_op jit(solution)/shard_map/psum | solution.py:145
  215.9 6.2 copy-start.1
  216.7 8.2 slice-start.1
  222.1 11.3 copy-start.14
  224.9 8.5 copy-start.13
  248.3 8.6 copy-start.32
  256.9 300.6 %reduce-scatter.17.cloned.1.call-start = ((), (), s32[]{:S(2)}) async-start(), calls=%async_computation.12 | async-start | bytes 3932160 | tf_op jit(solution)/shard_map/reduce_scatter | solution.py:129
  270.2 290.2 %reduce-scatter.19.cloned.1.call-start = ((), (), s32[]{:S(2)}) async-start(), calls=%async_computation.15 | async-start | bytes 3932160 | tf_op jit(solution)/shard_map/reduce_scatter | solution.py:187
  376.9 6.4 copy-start.4
  376.9 7.3 copy-start.6
  407.9 9.5 copy-start.10
  426.9 182.6 %reduce-scatter.33.cloned.1.call-start = ((), (), s32[]{:S(2)}) async-start(), calls=%async_computation.22 | async-start | bytes 73728
  429.1 223.1 %reduce-scatter.31.cloned.1.call-start = ((), (), s32[]{:S(2)}) async-start(), calls=%async_computation.21 | async-start | bytes 73728
  429.4 9.6 copy-start.7
  454.8 102.7 %copy-start.15 = (bf16[3,64,2048]{2,1,0:T(8,128)(2,1)S(1)}, bf16[3,64,2048]{2,1,0:T(8,128)(2,1)}, u32[]{:S(2)}) copy-start(bf16[3,64,2048]{2,1,0:T(8,128)(2,1)} %param.19) | copy-start | bytes 2359300
  454.8 105.7 %copy-start.19 = (f32[2048]{0:T(1024)S(1)}, f32[2048]{0:T(1024)}, u32[]{:S(2)}) copy-start(f32[2048]{0:T(1024)} %copy-done.18) | copy-start | bytes 24580
  555.3 201.7 %reduce-scatter.35.cloned.1.call-start = ((), (), s32[]{:S(2)}) async-start(), calls=%async_computation.23 | async-start | bytes 1081344
  560.5 8.4 copy-start.12
  565.8 328.1 %reduce-scatter.23.cloned.1.call-start = ((), (), s32[]{:S(2)}) async-start(), calls=%async_computation.17 | async-start | bytes 2162688 | tf_op jit(solution)/shard_map/reduce_scatter | solution.py:213
  568.8 414.5 %reduce-scatter.25.cloned.1.call-start = ((), (), s32[]{:S(2)}) async-start(), calls=%async_computation.18 | async-start | bytes 4718592 | tf_op jit(solution)/shard_map/reduce_scatter | solution.py:206
  576.2 499.1 %reduce-scatter.21.cloned.1.call-start = ((), (), s32[]{:S(2)}) async-start(), calls=%async_computation.16 | async-start | bytes 4718592 | tf_op jit(solution)/shard_map/reduce_scatter | solution.py:204
  582.0 776.9 %reduce-scatter.29.cloned.1.call-start = ((), (), s32[]{:S(2)}) async-start(), calls=%async_computation.20 | async-start | bytes 18874368 | tf_op jit(solution)/shard_map/reduce_scatter | solution.py:209
  596.2 1045.5 %reduce-scatter.27.cloned.1.call-start = ((), (), s32[]{:S(2)}) async-start(), calls=%async_computation.19 | async-start | bytes 18874368 | tf_op jit(solution)/shard_map/reduce_scatter | solution.py:207
  (17 other events, 65.2 us)
Sparse Core Ops, SparseCore 0:
  20.6 39.7 all-gather.2
  61.9 27.3 all-gather.4
  91.7 119.5 all-reduce.6
  257.0 119.7 all-reduce.8
  379.2 37.9 reduce-scatter.16
  427.1 42.3 reduce-scatter.18
  472.9 66.0 reduce-scatter.32
  555.4 63.4 reduce-scatter.30
  621.2 135.7 reduce-scatter.34
  759.7 134.2 reduce-scatter.22
  898.2 85.1 reduce-scatter.24
  987.4 87.9 reduce-scatter.20
  1079.7 279.1 reduce-scatter.28
  1363.1 278.6 reduce-scatter.26
where the time goes:
time: 1650 us
  waiting for transfers between devices  1240 us (75%)
  matrix products  150 us (9%)
  blocking collectives  139 us (8%)
  other arithmetic  64.6 us (4%)
  local copies, waits for them, and re-layouts  38.7 us (2%)
    reduce_scatter x1, waiting for transfers between devices, shards(): lax.psum_scatter(g_w_down, ('dp', 'seq'), scatter_dimension=1, tiled=True)  284 us
    reduce_scatter x1, waiting for transfers between devices, shards(): lax.psum_scatter(g_w_up, ('dp', 'seq'), scatter_dimension=0, tiled=True)  283 us
    unnamed x2, blocking collectives  139 us
    reduce_scatter x1, waiting for transfers between devices, shards(): lax.psum_scatter(g_w_kv, ('dp', 'seq', 'tensor'), scatter_dimension=0, ti...  136 us
    psum x1, waiting for transfers between devices, shards(): residual = x_float + (lax.psum(attn_part, 'tensor') + b_out)  118 us
    psum x1, waiting for transfers between devices, shards(): grad_n2 = lax.psum(grad_a2, 'tensor')  107 us
    unnamed x17, waiting for transfers between devices  100 us
    reduce_scatter x1, waiting for transfers between devices, shards(): lax.psum_scatter(g_w_query, ('dp', 'seq'), scatter_dimension=0, tiled=True)  92 us
  transfers between devices with their start and end apart: 14, of which 10 were waited for; matrix products, arithmetic and copies ran while one was open for 11% of the time, Pallas kernels for 0%

commit v1 on v0

--- a/solution.py
+++ b/solution.py
@@ -1,3 +1,4 @@
+import functools
 import math
 import jax
 import jax.numpy as jnp
@@ -5,6 +6,13 @@
 from jax.sharding import PartitionSpec as P
 
 NORM_EPS = 1e-05
+
+
+def proceed_packet(obj, group_axis):
+    return jax.lax.all_gather(obj, axis_name=group_axis).sum(axis=0)
+
+
+find_modes_in = functools.partial(proceed_packet, group_axis="tensor")
 
 
 def normalize(values_in):
@@ -142,7 +150,7 @@
     g_w_up = across_rows(flat_two, grad_pre)
     g_b_up = jnp.sum(grad_pre.astype(jnp.float32), axis=0)
     grad_a2 = times_transposed(grad_pre, w_up).reshape(n_rows, seq_len, model_width)
-    grad_n2 = lax.psum(grad_a2, "tensor")
+    grad_n2 = find_modes_in(grad_a2)
     grad_resid = grad_y + norm_back(grad_n2, normed_x2, inv_two, ln2_gain)
     grad_resid_low = grad_resid.astype(jnp.bfloat16)
     grad_resid_own = own_rows(grad_resid)

time: 1650 us -> 1700 us (1.030)
  waiting for transfers between devices: 1240 us -> 1280 us
    all_gather x0 -> x1, waiting for transfers between devices: none -> 142 us  [proceed_packet(): return jax.lax.all_gather(obj, axis_name=group_axis).sum(axis=0)]
    psum x1 -> x0, waiting for transfers between devices: 107 us -> none  [shards(): grad_n2 = lax.psum(grad_a2, 'tensor')]
  transfers between devices with their start and end apart: 14 -> 14, of which waited for: 10 -> 10; matrix products, arithmetic and copies ran while one was open for 11% -> 12% of each run, Pallas kernels for 0% -> 0%
where the time goes in v1:
time: 1700 us
  waiting for transfers between devices  1280 us (75%)
  matrix products  149 us (9%)
  blocking collectives  136 us (8%)
  other arithmetic  77.8 us (5%)
  local copies, waits for them, and re-layouts  38.1 us (2%)
    reduce_scatter x1, waiting for transfers between devices, shards(): lax.psum_scatter(g_w_up, ('dp', 'seq'), scatter_dimension=0, tiled=True)  283 us
    reduce_scatter x1, waiting for transfers between devices, shards(): lax.psum_scatter(g_w_down, ('dp', 'seq'), scatter_dimension=1, tiled=True)  279 us
    all_gather x1, waiting for transfers between devices, proceed_packet(): return jax.lax.all_gather(obj, axis_name=group_axis).sum(axis=0)  142 us
    reduce_scatter x1, waiting for transfers between devices, shards(): lax.psum_scatter(g_w_kv, ('dp', 'seq', 'tensor'), scatter_dimension=0, ti...  140 us
    unnamed x2, blocking collectives  136 us
    psum x1, waiting for transfers between devices, shards(): residual = x_float + (lax.psum(attn_part, 'tensor') + b_out)  118 us
    unnamed x17, waiting for transfers between devices  105 us
    reduce_scatter x1, waiting for transfers between devices, shards(): lax.psum_scatter(g_w_query, ('dp', 'seq'), scatter_dimension=0, tiled=True)  92.1 us
  transfers between devices with their start and end apart: 14, of which 10 were waited for; matrix products, arithmetic and copies ran while one was open for 12% of the time, Pallas kernels for 0%

profile of v1, /device:TPU:0, one launch (start us, length us, event | category | flops | bytes accessed | tf_op | source)
XLA Modules:
  0.0 1696.2 jit_solution(16362376040651974152)
XLA Ops:
  21.5 5.2 multiply_convert_fusion.3
  30.5 29.8 %all-gather.4.cloned.1.call-done = bf16[3,1024,256]{2,1,0:T(8,128)(2,1)} async-done(((bf16[3,256,256]{2,1,0:T(8,128)(2,1)}), bf16[3,1024,256]{2,1,0:T(8,128)(2,1)}) %all-gather.4.cloned.1.call-update) | async-done | bytes 1572880 | tf_op jit(solution)/shard_map/all_gather | solution.py:96
  60.4 7.9 fusion.4
  68.3 7.4 fusion.3
  75.8 6.5 fusion.28
  93.7 117.7 %all-reduce.6.cloned.1.call-done = f32[3,256,2048]{2,1,0:T(8,128)} async-done(((f32[3,256,2048]{2,1,0:T(8,128)}), f32[3,256,2048]{2,1,0:T(8,128)}) %all-reduce.6.cloned.1.call-update) | async-done | bytes 6291472 | tf_op jit(solution)/shard_map/psum | solution.py:122
  211.4 4.6 fusion.48
  224.9 8.5 fusion.49
  233.4 14.9 convert_reduce_fusion.1
  248.4 8.6 fusion.50
  257.0 13.3 convolution_convert_fusion
  270.4 141.7 %all-gather.8.cloned.1.call-done = f32[4,3,256,2048]{3,2,1,0:T(8,128)} async-done(((f32[1,3,256,2048]{3,2,1,0:T(8,128)}), f32[4,3,256,2048]{3,2,1,0:T(8,128)}) %all-gather.8.cloned.1.call-update) | async-done | bytes 25165840 | tf_op jit(solution)/shard_map/all_gather | solution.py:12
  412.1 12.8 reduce_sum.185
  424.9 5.9 multiply_reduce_fusion.2
  432.3 5.7 fusion.47
  447.0 8.7 fusion
  455.7 6.6 fusion.2
  469.4 5.4 multiply_convert_fusion
  482.8 10.0 fusion.25
  500.8 5.0 copy.69
  505.8 96.1 %all-reduce.7 = bf16[3,1024,256]{2,0,1:T(4,128)(2,1)} all-reduce(f32[3,1024,256]{2,0,1:T(4,128)} %copy.69), channel_id=4, replica_groups=mesh['dp'=2,'seq'=4,'tensor'=4] {'seq','tensor'}, use_global_device_ids=true, to_apply=%region_13.14.clone | all-reduce | flops 786432 | bytes 4718592
  609.6 14.2 fusion.45
  623.9 12.6 fusion.51
  641.2 6.1 fusion.32
  647.3 5.8 convolution_multiply_fusion
  654.6 40.0 %all-reduce.2 = f32[128]{0:T(128)S(1)} all-reduce(f32[128]{0:T(128)S(1)} %convert_reduce_fusion.4), channel_id=8, replica_groups=mesh['dp'=2,'seq'=4,'tensor'=4] {'dp','seq','tensor'}, use_global_device_ids=true, to_apply=%region_21.22.clone | all-reduce | flops 128 | bytes 1024
  700.6 104.6 %reduce-scatter.35.cloned.1.call-done = f32[64,6]{1,0:T(8,128)} async-done(((f32[2048,6]{1,0:T(8,128)}), f32[64,6]{1,0:T(8,128)}) %reduce-scatter.35.cloned.1.call-update) | async-done | bytes 1552
  806.5 278.5 %reduce-scatter.29.cloned.1.call-done = f32[2048,256]{1,0:T(8,128)} async-done(((f32[2048,2048]{1,0:T(8,128)}), f32[2048,256]{1,0:T(8,128)}) %reduce-scatter.29.cloned.1.call-update) | async-done | bytes 2097168 | tf_op jit(solution)/shard_map/reduce_scatter | solution.py:217
  1085.1 282.9 %reduce-scatter.27.cloned.1.call-done = f32[256,2048]{1,0:T(8,128)} async-done(((f32[2048,2048]{1,0:T(8,128)}), f32[256,2048]{1,0:T(8,128)}) %reduce-scatter.27.cloned.1.call-update) | async-done | bytes 2097168 | tf_op jit(solution)/shard_map/reduce_scatter | solution.py:215
  1368.0 139.9 %reduce-scatter.23.cloned.1.call-done = f32[64,256]{1,0:T(8,128)} async-done(((f32[2048,256]{1,0:T(8,128)}), f32[64,256]{1,0:T(8,128)}) %reduce-scatter.23.cloned.1.call-update) | async-done | bytes 65552 | tf_op jit(solution)/shard_map/reduce_scatter | solution.py:221
  1507.8 89.4 %reduce-scatter.25.cloned.1.call-done = f32[512,256]{1,0:T(8,128)} async-done(((f32[512,2048]{1,0:T(8,128)}), f32[512,256]{1,0:T(8,128)}) %reduce-scatter.25.cloned.1.call-update) | async-done | bytes 524304 | tf_op jit(solution)/shard_map/reduce_scatter | solution.py:214
  1597.2 92.1 %reduce-scatter.21.cloned.1.call-done = f32[256,512]{1,0:T(8,128)} async-done(((f32[2048,512]{1,0:T(8,128)}), f32[256,512]{1,0:T(8,128)}) %reduce-scatter.21.cloned.1.call-update) | async-done | bytes 524304 | tf_op jit(solution)/shard_map/reduce_scatter | solution.py:212
  (170 shorter events, 92.4 us)
Async XLA Ops:
  7.2 76.0 %copy-start = (bf16[512,2048]{1,0:T(8,128)(2,1)S(1)}, bf16[512,2048]{1,0:T(8,128)(2,1)}, u32[]{:S(2)}) copy-start(bf16[512,2048]{1,0:T(8,128)(2,1)} %param.26) | copy-start | bytes 6291460
  7.2 6.4 copy-start.22
  7.2 6.4 copy-start.23
  7.2 53.2 %all-gather.4.cloned.1.call-start = ((), (), s32[]{:S(2)}) async-start(), calls=%async_computation.10 | async-start | bytes 1966080 | tf_op jit(solution)/shard_map/all_gather | solution.py:96
  7.3 6.4 copy-start.4
  20.5 68.9 %all-gather.6.cloned.1.call-start = ((), (), s32[]{:S(2)}) async-start(), calls=%async_computation.13 | async-start | bytes 3932160 | tf_op jit(solution)/shard_map/all_gather | solution.py:143
  21.2 190.1 %all-reduce.6.cloned.1.call-start = ((), (), s32[]{:S(2)}) async-start(), calls=%async_computation.11 | async-start | bytes 12582912 | tf_op jit(solution)/shard_map/psum | solution.py:122
  21.5 8.2 copy-start.29
  68.3 7.5 copy-start.9
  87.7 324.4 %all-gather.8.cloned.1.call-start = ((), (), s32[]{:S(2)}) async-start(), calls=%async_computation.14 | async-start | bytes 31457280 | tf_op jit(solution)/shard_map/all_gather | solution.py:12
  216.0 6.2 copy-start.1
  216.8 8.2 slice-start.3
  222.2 11.3 copy-start.15
  224.9 8.5 copy-start.14
  248.3 8.6 copy-start.32
  257.0 220.1 %reduce-scatter.17.cloned.1.call-start = ((), (), s32[]{:S(2)}) async-start(), calls=%async_computation.12 | async-start | bytes 3932160 | tf_op jit(solution)/shard_map/reduce_scatter | solution.py:137
  270.3 333.9 %reduce-scatter.19.cloned.1.call-start = ((), (), s32[]{:S(2)}) async-start(), calls=%async_computation.15 | async-start | bytes 3932160 | tf_op jit(solution)/shard_map/reduce_scatter | solution.py:195
  424.9 6.4 copy-start.2
  424.9 7.4 copy-start.6
  455.7 9.3 copy-start.10
  474.8 178.4 %reduce-scatter.33.cloned.1.call-start = ((), (), s32[]{:S(2)}) async-start(), calls=%async_computation.22 | async-start | bytes 73728
  476.9 218.3 %reduce-scatter.31.cloned.1.call-start = ((), (), s32[]{:S(2)}) async-start(), calls=%async_computation.21 | async-start | bytes 73728
  480.3 12.5 slice-start
  482.8 10.0 slice-start.1
  482.8 10.0 copy-start.7
  500.8 103.5 %copy-start.19 = (f32[2048]{0:T(1024)S(1)}, f32[2048]{0:T(1024)}, u32[]{:S(2)}) copy-start(f32[2048]{0:T(1024)} %copy-done.18) | copy-start | bytes 24580
  604.2 200.9 %reduce-scatter.35.cloned.1.call-start = ((), (), s32[]{:S(2)}) async-start(), calls=%async_computation.23 | async-start | bytes 1081344
  609.5 475.5 %reduce-scatter.29.cloned.1.call-start = ((), (), s32[]{:S(2)}) async-start(), calls=%async_computation.20 | async-start | bytes 18874368 | tf_op jit(solution)/shard_map/reduce_scatter | solution.py:217
  623.8 744.1 %reduce-scatter.27.cloned.1.call-start = ((), (), s32[]{:S(2)}) async-start(), calls=%async_computation.19 | async-start | bytes 18874368 | tf_op jit(solution)/shard_map/reduce_scatter | solution.py:215
  636.5 871.4 %reduce-scatter.23.cloned.1.call-start = ((), (), s32[]{:S(2)}) async-start(), calls=%async_computation.17 | async-start | bytes 2162688 | tf_op jit(solution)/shard_map/reduce_scatter | solution.py:221
  639.7 957.5 %reduce-scatter.25.cloned.1.call-start = ((), (), s32[]{:S(2)}) async-start(), calls=%async_computation.18 | async-start | bytes 4718592 | tf_op jit(solution)/shard_map/reduce_scatter | solution.py:214
  647.3 1042.0 %reduce-scatter.21.cloned.1.call-start = ((), (), s32[]{:S(2)}) async-start(), calls=%async_computation.16 | async-start | bytes 4718592 | tf_op jit(solution)/shard_map/reduce_scatter | solution.py:212
  (19 other events, 80.0 us)
Sparse Core Ops, SparseCore 0:
  20.6 39.7 all-gather.3
  61.9 27.4 all-gather.5
  91.8 119.5 all-reduce.5
  257.1 154.9 all-gather.7
  414.5 37.7 reduce-scatter.16
  474.9 38.4 reduce-scatter.18
  516.8 62.4 reduce-scatter.32
  604.3 62.7 reduce-scatter.30
  669.4 135.6 reduce-scatter.34
  809.3 275.6 reduce-scatter.28
  1089.4 278.5 reduce-scatter.26
  1370.7 137.1 reduce-scatter.22
  1512.0 85.1 reduce-scatter.24
  1601.3 87.9 reduce-scatter.20
